TPU v7x, 512 devices: a whole 4x8x8 slice. The times are simulated.
512 devices in a mesh: replica: 8 (over y_lo, core), shard: 64 (over z, y_hi, x).
Axes of the slice: x: 4, y: 8 (y_hi: 2, y_lo: 4; y = y_hi * 4 + y_lo), z: 8, core: 2. Of those that a mesh axis runs over, the one named last changes fastest.
Arguments:
- gradients: bfloat16 [8, 2, 64, 1024, 256], P('replica', None, None, 'shard'), may hold values from -36 to 36
- momentum: float32 [8, 64, 1024, 256], P('replica', None, 'shard'), may hold values from -3 to 3
- params: float32 [64, 1024, 256], P(None, ('shard', 'replica')), may hold values from -6 to 6
- outer_moment: float32 [64, 1024, 256], P(None, ('shard', 'replica')), may hold values from -2 to 2
- shadow: float32 [64, 1024, 256], P(None, ('shard', 'replica')), may hold values from -6 to 6
Outputs:
- new_params: float32 [64, 1024, 256], P(None, ('shard', 'replica'))
- new_outer_moment: float32 [64, 1024, 256], P(None, ('shard', 'replica'))
- new_shadow: float32 [64, 1024, 256], P(None, ('shard', 'replica'))
- new_momentum: float32 [8, 64, 1024, 256], P('replica', None, 'shard')
All inputs are finite; a program needn't handle non-finite values.
Results may differ from a plain program's by a relative error of at most 0.0085.
Values may be sent and summed in bfloat16 or wider, within the bound.
A program may use at most 64 MiB of HBM per device.

v0:
```python
import math
import jax
import jax.numpy as jnp
from jax import lax
from jax.sharding import PartitionSpec as P

D = 1024
INNER = 2
NS_ITERS = 5
quintic_a = 3.4445
quintic_b = -4.775
quintic_c = 2.0315
inner_beta = 0.95
outer_mu = 0.9
outer_rate = 0.7
shadow_decay = 0.9


def split_up(shard, dim, size):
    before, after = (shard.shape[:dim], shard.shape[dim + 1 :])
    return jnp.moveaxis(shard.reshape(*before, size, -1, *after), dim, 0)


def sum_at_owner(shard, axis, dim):
    size = lax.axis_size(axis)
    tiles = lax.all_to_all(split_up(shard, dim, size), axis, 0, 0, tiled=True)
    return jnp.sum(tiles.astype(jnp.float32), axis=0)


def newton_schulz(blocks):
    squares = jnp.sum(jnp.square(blocks.astype(jnp.float32)), axis=(1, 2), keepdims=True)
    current = (blocks.astype(jnp.float32) / (jnp.sqrt(squares) + 1e-07)).astype(jnp.bfloat16)
    for repeat in range(NS_ITERS):
        gram_block = jnp.einsum(
            "mdi,mdj->mij", current, current, preferred_element_type=jnp.float32
        ).astype(jnp.bfloat16)
        square = jnp.einsum(
            "mij,mjk->mik", gram_block, gram_block, preferred_element_type=jnp.float32
        )
        polynomial = (quintic_b * gram_block.astype(jnp.float32) + quintic_c * square).astype(
            jnp.bfloat16
        )
        product = jnp.einsum(
            "mdi,mij->mdj", current, polynomial, preferred_element_type=jnp.float32
        )
        current = (quintic_a * current.astype(jnp.float32) + product).astype(jnp.bfloat16)
    return current


def body(gradients, momentum, params, outer_moment, shadow):
    scale_step = 0.2 * math.sqrt(D)
    shard_count = lax.axis_size("shard")
    replica_count = lax.axis_size("replica")
    moment_now = momentum[0]
    updates = []
    for position in range(INNER):
        grad_now = gradients[0, position].astype(jnp.float32)
        moment_now = inner_beta * moment_now + grad_now
        updates.append((grad_now + inner_beta * moment_now).astype(jnp.bfloat16))
    owned_total = None
    stacked = jnp.stack(updates)
    owned = lax.all_to_all(stacked, "shard", split_axis=1, concat_axis=2, tiled=True)
    orthos = newton_schulz(owned.reshape((-1,) + owned.shape[2:])).reshape(owned.shape)
    owned_total = scale_step * orthos[0].astype(jnp.float32)
    position = 1
    owned_total = owned_total + scale_step * orthos[position].astype(jnp.float32)
    mat_count = owned_total.shape[0]
    rows_each = owned_total.shape[1] // (shard_count * replica_count)
    width = owned_total.shape[2]
    grouped = owned_total.reshape((mat_count, shard_count, replica_count, rows_each, width))
    reduced = sum_at_owner(grouped.astype(jnp.bfloat16), "replica", 2)
    reduced = reduced.reshape((mat_count, shard_count, rows_each, width))
    placed = lax.all_to_all(
        reduced.astype(jnp.bfloat16), "shard", split_axis=1, concat_axis=0, tiled=True
    ).astype(reduced.dtype)
    summed = placed.reshape((mat_count * shard_count, rows_each, width))
    outer_delta = summed / replica_count
    new_outer = outer_mu * outer_moment + outer_delta
    new_params = params - outer_rate * (outer_delta + outer_mu * new_outer)
    new_shadow = shadow_decay * shadow + (1.0 - shadow_decay) * new_params
    return (new_params, new_outer, new_shadow, moment_now[None])


def solution(mesh):
    in_specs = (
        P("replica", None, None, "shard", None),
        P("replica", None, "shard", None),
        P(None, ("shard", "replica"), None),
        P(None, ("shard", "replica"), None),
        P(None, ("shard", "replica"), None),
    )
    out_specs = (
        P(None, ("shard", "replica"), None),
        P(None, ("shard", "replica"), None),
        P(None, ("shard", "replica"), None),
        P("replica", None, "shard", None),
    )
    return jax.shard_map(body, mesh=mesh, in_specs=in_specs, out_specs=out_specs, check_vma=False)
```

profile of v0, /device:TPU:2, one launch (start us, length us, event | category | flops | bytes accessed | tf_op | source)
XLA Modules:
  0.0 101.9 jit_solution(3864957524999742524)
XLA Ops:
  0.6 2.9 %fusion.14 = (f32[1,64,16,256]{3,2,1,0:T(8,128)}, bf16[1,64,16,256]{3,2,0,1:T(8,128)(2,1)S(1)}, bf16[1,64,16,256]{3,2,0,1:T(8,128)(2,1)S(1)}) fusion(f32[1,64,16,256]{3,2,1,0:T(8,128)} %param.6, bf16[1,2,64,16,256]{4,3,2,1,0:T(8,128)(2,1)} %param.5), kind=kLoop, calls=%fused_computation.38 | loop fusion | flops 2883584 | bytes 4194304
  3.5 0.1 pad_maximum_fusion
  3.6 46.8 %all_to_all.23 = bf16[2,64,16,256]{3,2,0,1:T(8,128)(2,1)S(1)} all-to-all(bf16[2,64,16,256]{3,2,0,1:T(8,128)(2,1)S(1)} %pad_maximum_fusion), channel_id=1, replica_groups=mesh['replica'=8,'shard'=64] {'shard'}, dimensions={1} | all-to-all | bytes 2097152 | tf_op jit(solution)/shard_map/all_to_all | solution.py:62
  50.4 0.4 multiply_reduce_fusion
  50.8 0.3 copy.15
  51.1 0.2 fusion
  51.3 0.5 convolution_convert_fusion.4
  51.9 0.6 add_convert_fusion.4
  52.5 0.5 convolution_convert_fusion.3
  53.0 0.6 add_convert_fusion.3
  53.7 0.5 convolution_convert_fusion.2
  54.2 0.6 add_convert_fusion.2
  54.9 0.5 convolution_convert_fusion.1
  55.4 0.6 add_convert_fusion.1
  56.0 0.5 convolution_convert_fusion
  56.6 0.6 add_convert_fusion
  57.2 0.2 multiply_convert_fusion
  57.4 0.0 copy-start
  57.4 0.2 convert_element_type.209
  57.6 0.4 copy.29
  58.0 23.1 %all_to_all.24 = bf16[8,1,64,1,2,256]{5,4,2,3,1,0:T(2,128)(2,1)S(1)} all-to-all(bf16[8,1,64,1,2,256]{5,4,2,3,1,0:T(2,128)(2,1)S(1)} %bitcast.65), channel_id=1, replica_groups=mesh['replica'=8,'shard'=64] {'replica'}, dimensions={0} | all-to-all | bytes 1048576 | tf_op jit(solution)/shard_map/all_to_all | solution.py:26
  81.1 0.5 reduce_sum.22
  81.6 19.3 %all_to_all.25 = bf16[1,64,2,256]{3,2,0,1:T(2,128)(2,1)S(1)} all-to-all(bf16[1,64,2,256]{3,2,0,1:T(2,128)(2,1)S(1)} %bitcast.66), channel_id=1, replica_groups=mesh['replica'=8,'shard'=64] {'shard'}, dimensions={1} | all-to-all | bytes 131072 | tf_op jit(solution)/shard_map/all_to_all | solution.py:73
  100.9 1.0 multiply_add_fusion
  (6 shorter events, 0.0 us)
Async XLA Ops:
  57.4 43.5 %copy-start = (f32[64,2,256]{2,1,0:T(2,128)S(1)}, f32[64,2,256]{2,1,0:T(2,128)}, u32[]{:S(2)}) copy-start(f32[64,2,256]{2,1,0:T(2,128)} %param.9) | copy-start | bytes 393220
  57.4 43.5 %copy-start.1 = (f32[64,2,256]{2,1,0:T(2,128)S(1)}, f32[64,2,256]{2,1,0:T(2,128)}, u32[]{:S(2)}) copy-start(f32[64,2,256]{2,1,0:T(2,128)} %param.7) | copy-start | bytes 393220
  57.4 43.5 %copy-start.2 = (f32[64,2,256]{2,1,0:T(2,128)S(1)}, f32[64,2,256]{2,1,0:T(2,128)}, u32[]{:S(2)}) copy-start(f32[64,2,256]{2,1,0:T(2,128)} %param.8) | copy-start | bytes 393220
where the time goes:
time: 102 us
  blocking collectives  89.2 us (87%)
  matrix products  5.78 us (6%)
  other arithmetic  5.3 us (5%)
    all_to_all x1, blocking collectives, body(): lax.all_to_all(stacked, 'shard', split_axis=1, concat_axis=2, tiled=True)  46.8 us
    all_to_all x1, blocking collectives, sum_at_owner(): tiles = lax.all_to_all(split_up(shard, dim, size), axis, 0, 0, tiled=True)  23.1 us
    all_to_all x1, blocking collectives, body(): lax.all_to_all(reduced.astype(jnp.bfloat16), 'shard', split_axis=1, conca...  19.3 us
    dot_general x5, matrix products, newton_schulz(): jnp.einsum('mdi,mij->mdj', current, polynomial, preferred_element_type=jn...  3.18 us
    unnamed x1, other arithmetic  2.85 us
    dot_general x5, matrix products, newton_schulz(): jnp.einsum('mdi,mdj->mij', current, current, preferred_element_type=jnp.f...  2.6 us

commit v1 on v0

--- a/solution.py
+++ b/solution.py
@@ -59,7 +59,12 @@
         updates.append((grad_now + inner_beta * moment_now).astype(jnp.bfloat16))
     owned_total = None
     stacked = jnp.stack(updates)
-    owned = lax.all_to_all(stacked, "shard", split_axis=1, concat_axis=2, tiled=True)
+    owned = jnp.concatenate(
+        lax.all_to_all(
+            jnp.stack(jnp.split(stacked, lax.axis_size("shard"), axis=1)), "shard", 0, 0
+        ),
+        axis=2,
+    )
     orthos = newton_schulz(owned.reshape((-1,) + owned.shape[2:])).reshape(owned.shape)
     owned_total = scale_step * orthos[0].astype(jnp.float32)
     position = 1

time: 102 us -> 103 us (level)
    convert_element_type x0 -> x2, other arithmetic: none -> 3.17 us  [the longest x1 2.89 us: body(): updates.append((grad_now + inner_beta * moment_now).astype(jnp.bfloat16))]
    unnamed x1 -> x63, other arithmetic: 2.85 us -> 0.23 us
where the time goes in v1:
time: 103 us
  blocking collectives  89.2 us (87%)
  matrix products  5.78 us (6%)
  other arithmetic  5.77 us (6%)
  between operations  1.26 us (1%)
    all_to_all x1, blocking collectives, body(): lax.all_to_all(jnp.stack(jnp.split(stacked, lax.axis_size('shard'), axis=...  46.8 us
    all_to_all x1, blocking collectives, sum_at_owner(): tiles = lax.all_to_all(split_up(shard, dim, size), axis, 0, 0, tiled=True)  23.1 us
    all_to_all x1, blocking collectives, body(): lax.all_to_all(reduced.astype(jnp.bfloat16), 'shard', split_axis=1, conca...  19.3 us
    dot_general x5, matrix products, newton_schulz(): jnp.einsum('mdi,mij->mdj', current, polynomial, preferred_element_type=jn...  3.18 us
    convert_element_type x1, other arithmetic, body(): updates.append((grad_now + inner_beta * moment_now).astype(jnp.bfloat16))  2.89 us
    dot_general x5, matrix products, newton_schulz(): jnp.einsum('mdi,mdj->mij', current, current, preferred_element_type=jnp.f...  2.61 us

profile of v1, /device:TPU:2, one launch (start us, length us, event | category | flops | bytes accessed | tf_op | source)
XLA Modules:
  0.0 102.8 jit_solution(5966478502687264438)
XLA Ops:
  0.6 2.9 %fusion.13 = (bf16[1,64,16,256]{3,2,1,0:T(8,128)(2,1)S(1)}, f32[1,64,16,256]{3,2,1,0:T(8,128)}, bf16[1,64,16,256]{3,2,1,0:T(8,128)(2,1)S(1)}) fusion(bf16[1,2,64,16,256]{4,3,2,1,0:T(8,128)(2,1)} %param.5, f32[1,64,16,256]{3,2,1,0:T(8,128)} %param.6), kind=kLoop, calls=%fused_computation.161 | loop fusion | flops 2883584 | bytes 4194304 | tf_op jit(solution)/shard_map/convert_element_type | solution.py:59
  4.2 46.8 %all_to_all.19 = bf16[64,2,1,16,256]{4,3,1,2,0:T(8,128)(2,1)S(1)} all-to-all(bf16[64,2,1,16,256]{4,3,1,2,0:T(8,128)(2,1)S(1)} %constant_dynamic-update-slice_fusion), channel_id=1, replica_groups=mesh['replica'=8,'shard'=64] {'shard'}, dimensions={0} | all-to-all | bytes 2097152 | tf_op jit(solution)/shard_map/all_to_all | solution.py:63
  51.1 0.4 fusion
  51.5 0.3 convert_bitcast_fusion
  51.8 0.2 copy.141
  52.0 0.3 divide_convert_fusion
  52.2 0.5 convolution_convert_fusion.4
  52.8 0.6 add_convert_fusion.4
  53.4 0.5 convolution_convert_fusion.3
  53.9 0.6 add_convert_fusion.3
  54.6 0.5 convolution_convert_fusion.2
  55.1 0.6 add_convert_fusion.2
  55.8 0.5 convolution_convert_fusion.1
  56.3 0.6 add_convert_fusion.1
  56.9 0.5 convolution_convert_fusion
  57.5 0.6 add_convert_fusion
  58.1 0.2 multiply_convert_fusion
  58.3 0.0 copy-start
  58.3 0.2 convert_element_type.213
  58.5 0.4 copy.217
  58.9 23.1 %all_to_all.20 = bf16[8,1,64,1,2,256]{5,4,2,3,1,0:T(2,128)(2,1)S(1)} all-to-all(bf16[8,1,64,1,2,256]{5,4,2,3,1,0:T(2,128)(2,1)S(1)} %bitcast.308), channel_id=1, replica_groups=mesh['replica'=8,'shard'=64] {'replica'}, dimensions={0} | all-to-all | bytes 1048576 | tf_op jit(solution)/shard_map/all_to_all | solution.py:26
  82.0 0.5 reduce_sum.22
  82.5 19.3 %all_to_all.21 = bf16[1,64,2,256]{3,2,0,1:T(2,128)(2,1)S(1)} all-to-all(bf16[1,64,2,256]{3,2,0,1:T(2,128)(2,1)S(1)} %bitcast.309), channel_id=1, replica_groups=mesh['replica'=8,'shard'=64] {'shard'}, dimensions={1} | all-to-all | bytes 131072 | tf_op jit(solution)/shard_map/all_to_all | solution.py:78
  101.8 1.0 multiply_add_fusion
  (70 shorter events, 0.3 us)
Async XLA Ops:
  58.3 43.5 %copy-start = (f32[64,2,256]{2,1,0:T(2,128)S(1)}, f32[64,2,256]{2,1,0:T(2,128)}, u32[]{:S(2)}) copy-start(f32[64,2,256]{2,1,0:T(2,128)} %param.9) | copy-start | bytes 393220
  58.3 43.5 %copy-start.1 = (f32[64,2,256]{2,1,0:T(2,128)S(1)}, f32[64,2,256]{2,1,0:T(2,128)}, u32[]{:S(2)}) copy-start(f32[64,2,256]{2,1,0:T(2,128)} %param.7) | copy-start | bytes 393220
  58.3 43.5 %copy-start.2 = (f32[64,2,256]{2,1,0:T(2,128)S(1)}, f32[64,2,256]{2,1,0:T(2,128)}, u32[]{:S(2)}) copy-start(f32[64,2,256]{2,1,0:T(2,128)} %param.8) | copy-start | bytes 393220
